TPU v7x, 32 devices: a whole 2x2x4 slice. The times are simulated.
32 devices in a mesh: tm: 4 (over y, x), rows: 8 (over z, core).
Axes of the slice: x: 2, y: 2, z: 4, core: 2. Of those that a mesh axis runs over, the one named last changes fastest.
Arguments:
- features: bfloat16 [48, 1280, 512], P('rows', 'tm'), may hold values from -6 to 6
- cotangent: bfloat16 [48, 1280, 512], P('rows', 'tm'), may hold values from -6 to 6
- state_bank: float32 [48, 512, 32], P('rows', 'tm'), may hold values from -6 to 6
- state_source: int32 [48], P('rows'), may hold values from 0 to 5, as said below
- master: float32 [88, 256, 256], P('tm', 'rows'), may hold values from -0.13258252 to 0.13258252
- left_stats: float32 [88, 256, 256], P('tm', 'rows'), may hold values from -7.68 to 64
- right_stats: float32 [88, 256, 256], P('tm', 'rows'), may hold values from -7.68 to 64
- left_root: float32 [88, 256, 256], P('tm', 'rows'), may hold values from -0.2 to 1.6
- right_root: float32 [88, 256, 256], P('tm'), may hold values from -0.2 to 1.6
- small_params: float32 [20, 512], replicated, may hold values from -1 to 1.5
- decay_logs: float32 [8, 32], P('tm'), may hold values from -7 to -1.5
- state_mix: float32 [2, 512, 32], P(None, 'tm'), may hold values from -0.6 to 0.6
Outputs:
- layer_out: bfloat16 [48, 1280, 512], P('rows', 'tm')
- grad_features: float32 [48, 1280, 512], P('rows', 'tm')
- grad_state: float32 [48, 512, 32], P('rows', 'tm')
- grad_blocks: float32 [88, 256, 256], P('tm', 'rows')
- new_left: float32 [88, 256, 256], P('tm', 'rows')
- new_right: float32 [88, 256, 256], P('tm', 'rows')
- new_master: float32 [88, 256, 256], P('tm', 'rows')
- new_copy: bfloat16 [88, 256, 256], P('tm', 'rows')
- grad_small: float32 [20, 512], P(None, 'tm')
- new_small: float32 [20, 512], P(None, 'tm')
- grad_decay: float32 [8, 32], P('tm')
- grad_mix: float32 [2, 512, 32], P(None, 'tm')
- new_decay: float32 [8, 32], P('tm')
- new_mix: float32 [2, 512, 32], P(None, 'tm')
Inputs may be any that keep to these rules, and one draw needn't show every extreme that they name: `state_source`: within each aligned block of 6 rows the values are a permutation of 0 to 5.
All inputs are finite; a program needn't handle non-finite values.
Results may differ from a plain program's by a relative error of at most 0.018.
Values may be sent and summed in bfloat16 or wider, within the bound.
A program may use at most 320 MiB of HBM per device.

v0:
```python
from functools import partial
import math
import jax
import jax.numpy as jnp
from jax import lax
from jax.sharding import PartitionSpec as P

D = 512
FF = 2048
NST = 32
KW = 15
BS = 256
precise = lax.Precision.HIGHEST
three_pass = lax.Precision.HIGH
rate_blocks = 0.1
rate_small = 0.5


def with_halo(block, sides, width):
    for axis, dim in sides:
        count = lax.axis_size(axis)
        forward = [(i, i + 1) for i in range(count - 1)]
        backward = [(target, source) for source, target in forward]
        low = lax.ppermute(
            lax.slice_in_dim(block, block.shape[dim] - width, None, axis=dim), axis, forward
        )
        high = lax.ppermute(lax.slice_in_dim(block, 0, width, axis=dim), axis, backward)
        block = jnp.concatenate([low, block, high], axis=dim)
    return block


def layer_norm(values, scales):
    center = values - jnp.mean(values, axis=-1, keepdims=True)
    spread = jnp.mean(center * center, axis=-1, keepdims=True)
    return center * lax.rsqrt(spread + 1e-05) * scales


def norm_back(values, scales, incoming):
    unused, pull_back = jax.vjp(layer_norm, values, scales)
    return pull_back(incoming)


def gating(values):
    half_width = values.shape[-1] // 2
    return values[..., :half_width] * jax.nn.sigmoid(values[..., half_width:])


def silu_back(values, incoming):
    return jax.vjp(jax.nn.silu, values)[1](incoming)[0]


def gating_back(values, incoming):
    return jax.vjp(gating, values)[1](incoming)[0]


def matmul(first, second):
    return jnp.dot(first, second, preferred_element_type=jnp.float32)


def inner_rows(first, second):
    return lax.dot_general(
        first, second, (((0,), (0,)), ((), ())), preferred_element_type=jnp.float32
    )


def inner_cols(first, second):
    return lax.dot_general(
        first, second, (((1,), (1,)), ((), ())), preferred_element_type=jnp.float32
    )


def to_matrix(block_stack, first, rows_count, cols_count):
    blocks_down = rows_count // BS
    blocks_across = cols_count // BS
    picked = block_stack[first : first + blocks_down * blocks_across]
    picked = picked.reshape(blocks_down, blocks_across, BS, BS).transpose(0, 2, 1, 3)
    return picked.reshape(rows_count, cols_count)


def to_blocks(matrix):
    rows_count, cols_count = matrix.shape
    return (
        matrix.reshape(rows_count // BS, BS, cols_count // BS, BS)
        .transpose(0, 2, 1, 3)
        .reshape(-1, BS, BS)
    )


def matrices(block_stack):
    ffn_count = D // BS * (FF // BS)
    mix_count = (D // BS) ** 2
    base_index = 4 * ffn_count
    return (
        to_matrix(block_stack, 0, D, FF),
        to_matrix(block_stack, ffn_count, FF, D),
        to_matrix(block_stack, 2 * ffn_count, D, FF),
        to_matrix(block_stack, 3 * ffn_count, FF, D),
        to_matrix(block_stack, base_index, D, D),
        to_matrix(block_stack, base_index + mix_count, D, 2 * D),
        to_matrix(block_stack, base_index + 3 * mix_count, D, 2 * D),
        to_matrix(block_stack, base_index + 5 * mix_count, D, D),
    )


def dft_tables(frames):
    period = 2 * frames - 1
    counter = jnp.arange(frames, dtype=jnp.int32)
    phase = (counter[:, None] * counter[None, :] % period).astype(jnp.float32) * (
        2.0 * math.pi / period
    )
    cosine = jnp.cos(phase)
    sine = jnp.sin(phase)
    forward_table = jnp.concatenate([cosine, -sine], axis=1)
    table_high = forward_table.astype(jnp.bfloat16)
    table_rest = (forward_table - table_high.astype(jnp.float32)).astype(jnp.bfloat16)
    split_table = jnp.concatenate([table_high, table_rest], axis=1)
    weighting = jnp.where(counter == 0, 1.0, 2.0).astype(jnp.float32) / period
    inverse_table = jnp.concatenate(
        [cosine * weighting[:, None], -sine * weighting[:, None]], axis=0
    )
    return (forward_table, split_table, inverse_table)


def conv_local(
    inputs_here,
    bank_rows,
    log_rates,
    mix_terms,
    selector,
    forward_table,
    split_table,
    inverse_table,
):
    row_count, frames, width = inputs_here.shape
    head_count = log_rates.shape[0]
    decay_rates = jnp.exp(log_rates)
    positions = jnp.arange(frames, dtype=jnp.float32)
    decay_now = jnp.exp(-decay_rates[:, :, None] * positions)
    decay_next = jnp.exp(-decay_rates[:, :, None] * (positions + 1.0))
    coupling = (mix_terms[0] * mix_terms[1]).reshape(head_count, width // head_count, NST)
    kernel = jnp.einsum("hdn,hnt->hdt", coupling, decay_now, precision=precise).reshape(
        width, frames
    )
    kernel_hat = jnp.dot(kernel, forward_table, precision=precise)
    both_hat = jnp.einsum(
        "rtc,tk->rck",
        inputs_here.astype(jnp.bfloat16),
        split_table,
        preferred_element_type=jnp.float32,
    )
    input_hat = both_hat[..., : 2 * frames] + both_hat[..., 2 * frames :]
    real_in = input_hat[..., :frames]
    imag_in = input_hat[..., frames:]
    real_kernel = kernel_hat[:, :frames]
    imag_kernel = kernel_hat[:, frames:]
    output_hat = jnp.concatenate(
        [
            real_in * real_kernel - imag_in * imag_kernel,
            real_in * imag_kernel + imag_in * real_kernel,
        ],
        axis=-1,
    )
    mixed = jnp.einsum("rck,kt->rtc", output_hat, inverse_table, precision=three_pass)
    starts = jnp.einsum("rs,scn->rcn", selector, bank_rows, precision=precise)
    carried = (mix_terms[1][None] * starts).reshape(row_count, head_count, width // head_count, NST)
    carried_out = jnp.einsum("rhdn,hnt->rthd", carried, decay_next, precision=precise)
    return mixed + carried_out.reshape(row_count, frames, width)


def ffn_forward(values, scales, weight_in, weight_out):
    normed = layer_norm(values, scales).astype(jnp.bfloat16)
    inner = matmul(normed, weight_in)
    activated = jax.nn.silu(inner).astype(jnp.bfloat16)
    return (0.5 * matmul(activated, weight_out), (normed, inner, activated))


def ffn_backward(values, scales, weight_in, weight_out, saved, incoming):
    normed, inner, activated = saved
    grad_outer = (0.5 * incoming).astype(jnp.bfloat16)
    grad_weight_out = inner_rows(activated, grad_outer)
    grad_act = inner_cols(grad_outer, weight_out)
    grad_inner = silu_back(inner, grad_act).astype(jnp.bfloat16)
    grad_weight_in = inner_rows(normed, grad_inner)
    grad_normed = inner_cols(grad_inner, weight_in)
    grad_values, grad_scales = norm_back(values, scales, grad_normed)
    return (incoming + grad_values, grad_scales, grad_weight_in, grad_weight_out)


def body(
    features,
    cotangent,
    state_bank,
    state_source,
    master,
    left_stats,
    right_stats,
    left_root,
    right_root,
    small_params,
    decay_logs,
    state_mix,
):
    row_count, frame_count, width = features.shape
    token_count = row_count * frame_count
    margin = (KW - 1) // 2
    scaling = 1.0 / math.sqrt(token_count * lax.axis_size("tm") * lax.axis_size("rows"))
    copy_part = master.astype(jnp.bfloat16)
    partial_stack = lax.all_gather(copy_part, "rows", axis=1, tiled=True)
    block_stack = lax.all_gather(partial_stack, "tm", axis=0, tiled=True)
    ffa_in, ffa_out, ffb_in, ffb_out, mixer_in, mixer_out, conv_in, conv_out = matrices(block_stack)
    kernel_rows = small_params[5:]
    stream_zero = features.astype(jnp.float32).reshape(token_count, width)
    branch_one, saved_one = ffn_forward(stream_zero, small_params[0], ffa_in, ffa_out)
    stream_one = stream_zero + branch_one
    normed_mixer = layer_norm(stream_one, small_params[1]).astype(jnp.bfloat16)
    mixer_input = (
        matmul(normed_mixer, mixer_in).astype(jnp.bfloat16).reshape(row_count, frame_count, width)
    )
    channel_in = lax.all_to_all(mixer_input, "tm", split_axis=2, concat_axis=1, tiled=True)
    forward_table, split_table, inverse_table = dft_tables(channel_in.shape[1])
    selector = (state_source[:, None] == jnp.arange(row_count, dtype=jnp.int32)[None, :]).astype(
        jnp.float32
    )
    mixer_local = partial(
        conv_local,
        selector=selector,
        forward_table=forward_table,
        split_table=split_table,
        inverse_table=inverse_table,
    )
    channel_out, mixer_pull = jax.vjp(
        mixer_local, channel_in.astype(jnp.float32), state_bank, decay_logs, state_mix
    )
    mixer_result = lax.all_to_all(
        channel_out.astype(jnp.bfloat16), "tm", split_axis=1, concat_axis=2, tiled=True
    ).reshape(token_count, width)
    gated = matmul(mixer_result, mixer_out)
    stream_two = stream_one + gating(gated)
    normed_conv = layer_norm(stream_two, small_params[2]).astype(jnp.bfloat16)
    pointwise = matmul(normed_conv, conv_in)
    gated_units = gating(pointwise).astype(jnp.bfloat16).reshape(row_count, frame_count, width)
    padded = with_halo(gated_units, (("tm", 1),), margin)
    padded_full = padded.astype(jnp.float32)
    depthwise = kernel_rows[0] * padded_full[:, 0:frame_count]
    for offset in range(1, KW):
        depthwise = depthwise + kernel_rows[offset] * padded_full[:, offset : offset + frame_count]
    depth_flat = depthwise.reshape(token_count, width)
    activated_conv = jax.nn.silu(depth_flat).astype(jnp.bfloat16)
    stream_three = stream_two + matmul(activated_conv, conv_out)
    branch_four, saved_four = ffn_forward(stream_three, small_params[3], ffb_in, ffb_out)
    stream_four = stream_three + branch_four
    layer_out, out_pull = jax.vjp(layer_norm, stream_four, small_params[4])
    grad_four, grad_gain_out = out_pull(cotangent.astype(jnp.float32).reshape(token_count, width))
    grad_three, grad_gain_b, grad_fb_in, grad_fb_out = ffn_backward(
        stream_three, small_params[3], ffb_in, ffb_out, saved_four, grad_four
    )
    grad_conv_out = grad_three.astype(jnp.bfloat16)
    grad_weight_conv_out = inner_rows(activated_conv, grad_conv_out)
    grad_activated = inner_cols(grad_conv_out, conv_out)
    grad_depth = (
        silu_back(depth_flat, grad_activated)
        .astype(jnp.bfloat16)
        .reshape(row_count, frame_count, width)
    )
    grad_padded = with_halo(grad_depth, (("tm", 1),), margin).astype(jnp.float32)
    grad_depth_full = grad_depth.astype(jnp.float32)
    grad_units = kernel_rows[0] * grad_padded[:, 2 * margin : 2 * margin + frame_count]
    kernel_grads = [jnp.sum(grad_depth_full * padded_full[:, 0:frame_count], axis=(0, 1))]
    for offset in range(1, KW):
        grad_units = (
            grad_units
            + kernel_rows[offset]
            * grad_padded[:, 2 * margin - offset : 2 * margin - offset + frame_count]
        )
        kernel_grads.append(
            jnp.sum(grad_depth_full * padded_full[:, offset : offset + frame_count], axis=(0, 1))
        )
    grad_pointwise = gating_back(pointwise, grad_units.reshape(token_count, width)).astype(
        jnp.bfloat16
    )
    grad_weight_conv_in = inner_rows(normed_conv, grad_pointwise)
    grad_values, grad_gain_c = norm_back(
        stream_two, small_params[2], inner_cols(grad_pointwise, conv_in)
    )
    grad_two = grad_three + grad_values
    grad_gated = gating_back(gated, grad_two).astype(jnp.bfloat16)
    grad_weight_mixer_out = inner_rows(mixer_result, grad_gated)
    grad_mixer_frames = (
        inner_cols(grad_gated, mixer_out)
        .astype(jnp.bfloat16)
        .reshape(row_count, frame_count, width)
    )
    grad_channel_out = lax.all_to_all(
        grad_mixer_frames, "tm", split_axis=2, concat_axis=1, tiled=True
    )
    grad_channel_in, grad_state, grad_logs, grad_mix_terms = mixer_pull(
        grad_channel_out.astype(jnp.float32)
    )
    grad_input_frames = lax.all_to_all(
        grad_channel_in.astype(jnp.bfloat16), "tm", split_axis=1, concat_axis=2, tiled=True
    ).reshape(token_count, width)
    grad_weight_mixer_in = inner_rows(normed_mixer, grad_input_frames)
    grad_values, grad_gain_s = norm_back(
        stream_one, small_params[1], inner_cols(grad_input_frames, mixer_in)
    )
    grad_one = grad_two + grad_values
    grad_zero, grad_gain_a, grad_fa_in, grad_fa_out = ffn_backward(
        stream_zero, small_params[0], ffa_in, ffa_out, saved_one, grad_one
    )
    grad_stack = (
        jnp.concatenate(
            [
                to_blocks(grad_fa_in),
                to_blocks(grad_fa_out),
                to_blocks(grad_fb_in),
                to_blocks(grad_fb_out),
                to_blocks(grad_weight_mixer_in),
                to_blocks(grad_weight_mixer_out),
                to_blocks(grad_weight_conv_in),
                to_blocks(grad_weight_conv_out),
            ],
            axis=0,
        )
        * scaling
    )
    small_grads = (
        jnp.concatenate(
            [
                jnp.stack([grad_gain_a, grad_gain_s, grad_gain_c, grad_gain_b, grad_gain_out]),
                jnp.stack(kernel_grads),
            ],
            axis=0,
        )
        * scaling
    )
    rows_part = lax.psum_scatter(
        grad_stack.astype(jnp.bfloat16), "rows", scatter_dimension=1, tiled=True
    )
    owned, small_part = (
        lax.psum_scatter(rows_part, "tm", scatter_dimension=0, tiled=True).astype(jnp.float32),
        lax.psum_scatter(
            small_grads.astype(jnp.bfloat16), "tm", scatter_dimension=1, tiled=True
        ).astype(jnp.float32),
    )
    decay_sum, mix_sum, small_sum = lax.psum(
        (grad_logs * scaling, grad_mix_terms * scaling, small_part), "rows"
    )
    full_grad = lax.all_gather(owned.astype(jnp.bfloat16), "rows", axis=1, tiled=True).astype(
        owned.dtype
    )
    slice_rows = owned.shape[1]
    grad_columns = lax.dynamic_slice_in_dim(
        full_grad, lax.axis_index("rows") * slice_rows, slice_rows, 2
    )
    new_left = 0.5 * left_stats + 0.5 * jnp.einsum(
        "bik,bjk->bij", owned, full_grad, precision=precise
    )
    new_right = 0.5 * right_stats + 0.5 * jnp.einsum(
        "bki,bkj->bij", grad_columns, full_grad, precision=precise
    )
    left_side = jnp.einsum("bij,bjk->bik", left_root, full_grad, precision=precise)
    step_value = jnp.einsum("bik,bkl->bil", left_side, right_root, precision=precise)
    new_master = master - rate_blocks * step_value
    small_width = small_sum.shape[1]
    own_small = lax.dynamic_slice_in_dim(
        small_params, lax.axis_index("tm") * small_width, small_width, 1
    )
    new_small = own_small - rate_small * small_sum
    new_decay = decay_logs - rate_small * decay_sum
    new_mix = state_mix - rate_small * mix_sum
    return (
        layer_out.astype(jnp.bfloat16).reshape(row_count, frame_count, width),
        grad_zero.reshape(row_count, frame_count, width),
        grad_state,
        owned,
        new_left,
        new_right,
        new_master,
        new_master.astype(jnp.bfloat16),
        small_sum,
        new_small,
        decay_sum,
        mix_sum,
        new_decay,
        new_mix,
    )


def solution(mesh):
    return jax.shard_map(
        body,
        mesh=mesh,
        in_specs=(
            P("rows", "tm", None),
            P("rows", "tm", None),
            P("rows", "tm", None),
            P("rows"),
            P("tm", "rows", None),
            P("tm", "rows", None),
            P("tm", "rows", None),
            P("tm", "rows", None),
            P("tm", None, None),
            P(),
            P("tm", None),
            P(None, "tm", None),
        ),
        out_specs=(
            P("rows", "tm", None),
            P("rows", "tm", None),
            P("rows", "tm", None),
            P("tm", "rows", None),
            P("tm", "rows", None),
            P("tm", "rows", None),
            P("tm", "rows", None),
            P("tm", "rows", None),
            P(None, "tm"),
            P(None, "tm"),
            P("tm", None),
            P(None, "tm", None),
            P("tm", None),
            P(None, "tm", None),
        ),
        check_vma=False,
    )
```

profile of v0, /device:TPU:0, one launch (start us, length us, event | category | flops | bytes accessed | tf_op | source)
XLA Modules:
  0.0 1053.2 jit_solution(16982755594584130233)
XLA Ops:
  9.4 39.7 %all-gather.4.cloned.1.call-done = bf16[22,256,256]{2,1,0:T(8,128)(2,1)} async-done(((bf16[22,32,256]{2,1,0:T(8,128)(2,1)}), bf16[22,256,256]{2,1,0:T(8,128)(2,1)}) %all-gather.4.cloned.1.call-update) | async-done | bytes 2883600 | tf_op jit(solution)/shard_map/all_gather | solution.py:208
  70.0 26.9 %sine_negate_fusion = (f32[1280,1280]{1,0:T(8,128)S(1)}, f32[1280,1280]{1,0:T(8,128)S(1)}) fusion(), kind=kLoop, calls=%fused_computation.60 | loop fusion | flops 16384000 | bytes 13107200 | tf_op jit(solution)/shard_map/neg | solution.py:119
  111.4 52.3 %all-gather.6.cloned.1.call-done = bf16[88,256,256]{2,1,0:T(8,128)(2,1)} async-done(((bf16[22,256,256]{2,1,0:T(8,128)(2,1)}), bf16[88,256,256]{2,1,0:T(8,128)(2,1)}) %all-gather.6.cloned.1.call-update) | async-done | bytes 11534352 | tf_op jit(solution)/shard_map/all_gather | solution.py:209
  180.0 9.7 multiply_convert_fusion.2
  205.7 28.6 %broadcast_multiply_fusion.1 = (f32[1280,1280]{1,0:T(8,128)}, f32[1280,1280]{1,0:T(8,128)}) fusion(f32[1280]{0:T(1024)S(1)} %select_multiply_fusion), kind=kLoop, calls=%fused_computation.184 | loop fusion | flops 19660800 | bytes 13112320 | tf_op jit(solution)/shard_map/mul | solution.py:119
  246.9 16.8 %fusion.18 = f32[6,128,5120]{2,1,0:T(8,128)} fusion(bf16[6,1280,128]{2,1,0:T(8,128)(2,1)S(1)} %bitcast.422, bf16[1280,2560]{1,0:T(8,128)(2,1)} %subtract_convert_fusion, bf16[1280,2560]{1,0:T(8,128)(2,1)} %fusion.32), kind=kOutput, calls=%fused_computation.49 | convolution fusion | flops 10092544000 | bytes 30801920 | tf_op jit(solution)/shard_map/jvp(rtc,tk->rck)/dot_general | solution.py:145
  276.5 35.6 %fusion.73 = bf16[6,1280,128]{2,1,0:T(8,128)(2,1)S(1)} fusion(f32[6,1280,128]{2,1,0:T(8,128)S(1)} %copy-done.52, f32[6,128,1280]{2,1,0:T(8,128)} %get-tuple-element.127, f32[6,128,1280]{2,1,0:T(8,128)S(1)} %get-tuple-element.126, f32[1280,1280]{1,0:T(8,128)} %get-tuple-element.169, f32[1280,1280]{1,0:T(8,128)} %get-tuple-element.168), kind=kOutput, calls=%fused_computation.136 | convolution fusion | flops 15106703360 | bytes 26869760 | tf_op jit(solution)/shard_map/jvp(rck,kt->rtc)/dot_general | solution.py:163
  330.4 24.2 %all-to-all-done.1 = bf16[6,1280,128]{2,0,1:T(8,128)(2,1)S(1)} async-done(((bf16[6,1280,128]{2,0,1:T(8,128)(2,1)}), bf16[6,1280,128]{2,0,1:T(8,128)(2,1)S(1)}, u32[]{:S(2)}, u32[]{:S(2)}) %all-to-all-start.1) | async-done | bytes 1966112 | tf_op jit(solution)/shard_map/all_to_all | solution.py:234
  407.2 8.8 multiply_convert_fusion.9
  428.0 10.1 multiply_convert_fusion.1
  449.3 14.8 %fusion.2 = bf16[1920,2048]{1,0:T(8,128)(2,1)} fusion(f32[1920,2048]{1,0:T(8,128)} %get-tuple-element.179, bf16[2048,512]{0,1:T(8,128)(2,1)S(1)} %bitcast.412, f32[1920,512]{0,1:T(8,128)S(1)} %get-tuple-element.109, f32[1920]{0:T(1024)S(1)} %negate_multiply_fusion.4), kind=kOutput, calls=%fused_computation.21 | convolution fusion | flops 4068802560 | bytes 29629952 | tf_op jit(solution)/shard_map/dot_general | solution.py:67
  464.1 8.6 multiply_reduce_fusion.5
  560.7 9.6 fusion.120
  570.3 20.0 %all-to-all-done.2 = bf16[6,320,512]{1,0,2:T(8,128)(2,1)} async-done(((bf16[6,320,512]{1,0,2:T(8,128)(2,1)}), bf16[6,320,512]{1,0,2:T(8,128)(2,1)}, u32[]{:S(2)}, u32[]{:S(2)}) %all-to-all-start.2) | async-done | bytes 1966112 | tf_op jit(solution)/shard_map/all_to_all | solution.py:293
  599.4 14.3 %fusion.16 = f32[6,128,2560]{2,1,0:T(8,128)S(1)} fusion(f32[1280,1280]{1,0:T(8,128)} %get-tuple-element.169, f32[1280,1280]{1,0:T(8,128)} %get-tuple-element.168, bf16[6,1280,128]{1,2,0:T(8,128)(2,1)} %copy.214), kind=kOutput, calls=%fused_computation.46 | convolution fusion | flops 15102771200 | bytes 22937600 | tf_op jit(solution)/shard_map/transpose(jvp(rck,kt->rtc))/dot_general | solution.py:163
  623.9 21.3 %fusion.79 = bf16[6,1280,128]{1,2,0:T(8,128)(2,1)S(1)} fusion(bf16[1280,2560]{1,0:T(8,128)(2,1)} %subtract_convert_fusion, bf16[1280,2560]{1,0:T(8,128)(2,1)} %fusion.32, f32[6,128,2560]{2,1,0:T(8,128)} %pad_add_fusion), kind=kOutput, calls=%fused_computation.185 | convolution fusion | flops 10097459200 | bytes 22937600 | tf_op jit(solution)/shard_map/transpose(jvp(rtc,tk->rck))/dot_general | solution.py:145
  703.5 9.7 fusion.187
  723.9 17.8 %fusion.8 = (bf16[2048,1920]{0,1:T(8,128)(2,1)}, f32[1920,2048]{1,0:T(8,128)}) fusion(f32[1920,2048]{1,0:T(8,128)} %get-tuple-element.171, bf16[1920,512]{0,1:T(8,128)(2,1)S(1)} %multiply_convert_fusion.5, bf16[2048,512]{0,1:T(8,128)(2,1)S(1)} %bitcast.407), kind=kOutput, calls=%fused_computation.27 | convolution fusion | flops 4065853440 | bytes 43384832 | tf_op jit(solution)/shard_map/dot_general | solution.py:67
  741.8 10.7 %copy.263 = bf16[2048,1920]{1,0:T(8,128)(2,1)} copy(bf16[2048,1920]{0,1:T(8,128)(2,1)} %get-tuple-element.188) | data formatting | bytes 15728640 | tf_op jit(solution)/shard_map/dot_general | solution.py:61
  752.5 17.1 %multiply_reduce_fusion.9 = (f32[1920]{0:T(1024)S(1)}, f32[1920,512]{0,1:T(8,128)S(1)}) fusion(f32[1920,512]{0,1:T(8,128)} %copy.178, f32[1920]{0:T(1024)S(1)} %copy-done.98, f32[512]{0:T(512)S(1)} %bitcast.439, bf16[512,2048]{1,0:T(8,128)(2,1)S(1)} %bitcast.405, f32[1920,2048]{1,0:T(8,128)} %get-tuple-element.171, f32[1920,2048]{1,0:T(8,128)} %get-tuple-element.189), kind=kOutput, calls=%fused_computation.149 | convolution fusion | flops 4069783552 | bytes 41436160 | tf_op jit(solution)/shard_map/dot_general | solution.py:67
  798.0 120.9 %reduce-scatter.6.cloned.1.call-done = bf16[88,32,256]{2,1,0:T(8,128)(2,1)} async-done(((bf16[88,256,256]{2,1,0:T(8,128)(2,1)}), bf16[88,32,256]{2,1,0:T(8,128)(2,1)}) %reduce-scatter.6.cloned.1.call-update) | async-done | bytes 1441808 | tf_op jit(solution)/shard_map/reduce_scatter | solution.py:336
  919.1 27.1 %fusion.52 = (f32[512]{0:T(512)S(1)}, f32[512]{0:T(512)S(1)}, f32[512]{0:T(512)S(1)}, f32[512]{0:T(512)S(1)}, f32[512]{0:T(512)S(1)}, /*index=5*/f32[512]{0:T(51...) fusion(bf16[6,320,512]{2,1,0:T(8,128)(2,1)S(1)} %bitcast.352, ...), kind=kLoop, calls=%fused_computation.97 | loop fusion | flops 30466560 | bytes 60979200 | tf_op jit(solution)/shard_map/reduce_sum | solution.py:276
  968.7 16.2 %fusion.30 = f32[128,1280]{1,0:T(8,128)S(1)} fusion(f32[1280,1280]{1,0:T(8,128)} %copy-done.2, f32[1280,1280]{1,0:T(8,128)} %copy-done.3, f32[128,1280]{1,0:T(8,128)S(1)} %add_any.121, f32[128,1280]{1,0:T(8,128)S(1)} %add_any.120), kind=kOutput, calls=%fused_computation.66 | convolution fusion | flops 5036769280 | bytes 15073280 | tf_op jit(solution)/shard_map/transpose(jvp())/dot_general | solution.py:144
  998.7 29.4 %all-reduce.13 = (f32[20,128]{1,0:T(8,128)S(1)}, f32[2,32]{1,0:T(2,128)S(1)}, f32[2,128,32]{1,2,0:T(8,128)S(1)}) all-reduce(bf16[20,128]{1,0:T(8,128)(2,1)S(1)} %copy.265, f32[2,32]{1,0:T(2,128)S(1)} %multiply_multiply_fusion.5, f32[2,128,32]{1,2,0:T(8,128)S(1)} %add_multiply_fusion), channel_id=1, replica_groups=mesh['tm'=4,'rows'=8] {'rows'}, use_global_device_ids=true, to_apply=%region_43.44 | all-reduce | flops 10816 | bytes 81408 | tf_op jit(solution)/shard_map/psum | solution.py:345
  (517 shorter events, 446.5 us)
Async XLA Ops:
  7.2 1024.4 %copy-start = (f32[22,32,256]{2,1,0:T(8,128)S(1)}, f32[22,32,256]{2,1,0:T(8,128)}, u32[]{:S(2)}) copy-start(f32[22,32,256]{2,1,0:T(8,128)} %param.19) | copy-start | bytes 2162692
  7.2 42.0 %copy-start.84 = (f32[2,128,32]{1,2,0:T(8,128)S(1)}, f32[2,128,32]{1,2,0:T(8,128)}, u32[]{:S(2)}) copy-start(f32[2,128,32]{1,2,0:T(8,128)} %param.23) | copy-start | bytes 98308
  7.2 42.1 %copy-start.142 = (s32[6]{0:T(128)S(1)}, s32[6]{0:T(128)}, u32[]{:S(2)}) copy-start(s32[6]{0:T(128)} %param.15) | copy-start | bytes 76
  7.2 42.1 %copy-start.88 = (f32[6,128,32]{1,2,0:T(8,128)S(1)}, f32[6,128,32]{1,2,0:T(8,128)}, u32[]{:S(2)}) copy-start(f32[6,128,32]{1,2,0:T(8,128)} %param.14) | copy-start | bytes 294916
  7.2 43.2 %copy-start.26 = (bf16[6,320,512]{2,1,0:T(8,128)(2,1)S(1)}, bf16[6,320,512]{2,1,0:T(8,128)(2,1)}, u32[]{:S(2)}) copy-start(bf16[6,320,512]{2,1,0:T(8,128)(2,1)} %param.12) | copy-start | bytes 5898244
  7.3 41.9 %all-gather.4.cloned.1.call-start = ((), (), s32[]{:S(2)}) async-start(), calls=%async_computation.7 | async-start | bytes 3244032 | tf_op jit(solution)/shard_map/all_gather | solution.py:208
  9.4 154.3 %all-gather.6.cloned.1.call-start = ((), (), s32[]{:S(2)}) async-start(), calls=%async_computation.8 | async-start | bytes 14417920 | tf_op jit(solution)/shard_map/all_gather | solution.py:209
  67.5 127.3 %copy-start.116 = (f32[1,512]{1,0:T(1,128)}, f32[1,512]{1,0:T(1,128)S(1)}, u32[]{:S(2)}) copy-start(f32[1,512]{1,0:T(1,128)S(1)} %get-tuple-element.161) | copy-start | bytes 6148
  67.5 295.0 %copy-start.118 = (f32[1,512]{1,0:T(1,128)}, f32[1,512]{1,0:T(1,128)S(1)}, u32[]{:S(2)}) copy-start(f32[1,512]{1,0:T(1,128)S(1)} %get-tuple-element.159) | copy-start | bytes 6148
  104.9 165.9 %copy-start.45 = (f32[128,1280]{1,0:T(8,128)}, f32[128,1280]{1,0:T(8,128)S(1)}, u32[]{:S(2)}) copy-start(f32[128,1280]{1,0:T(8,128)S(1)} %get-tuple-element.139) | copy-start | bytes 1966084
  200.8 41.2 %all-to-all-start = ((bf16[6,320,512]{1,0,2:T(8,128)(2,1)}), bf16[6,320,512]{1,0,2:T(8,128)(2,1)}, u32[]{:S(2)}, u32[]{:S(2)}) async-start(bf16[6,320,512]{1,0,2:T(8,128)(2,1)} %copy.180), calls=%async_computation | async-start | bytes 6291456 | tf_op jit(solution)/shard_map/all_to_all | solution.py:219
  320.6 34.0 %all-to-all-start.1 = ((bf16[6,1280,128]{2,0,1:T(8,128)(2,1)}), bf16[6,1280,128]{2,0,1:T(8,128)(2,1)S(1)}, u32[]{:S(2)}, u32[]{:S(2)}) async-start(bf16[6,1280,128]{2,0,1:T(8,128)(2,1)} %copy.192), calls=%async_computation.1 | async-start | bytes 5242880 | tf_op jit(solution)/shard_map/all_to_all | solution.py:234
  375.5 30.9 %collective-permute-start = (bf16[6,7,512]{2,1,0:T(8,128)(2,1)}, bf16[6,7,512]{2,1,0:T(8,128)(2,1)S(1)}, u32[]{:S(2)}, u32[]{:S(2)}) collective-permute-start(bf16[6,7,512]{2,1,0:T(8,128)(2,1)} %get-tuple-element.137), channel_id=1, source_target_pairs={{0,8},{8,16},{16,24},{1,9},{9,17},{17,25},{2,10},{10,18},{18,26},{... | collective-permute-start | bytes 129032 | tf_op jit(solution)/shard_map/ppermute | solution.py:24
  378.9 27.6 %collective-permute-start.1 = (bf16[6,7,512]{2,1,0:T(8,128)(2,1)S(1)}, bf16[6,7,512]{2,1,0:T(8,128)(2,1)S(1)}, u32[]{:S(2)}, u32[]{:S(2)}) collective-permute-start(bf16[6,7,512]{2,1,0:T(8,128)(2,1)S(1)} %get-tuple-element.138), channel_id=1, source_target_pairs={{8,0},{16,8},{24,16},{9,1},{17,9},{25,17},{10,2},{18,10},{26,18},{... | collective-permute-start | bytes 129032 | tf_op jit(solution)/shard_map/ppermute | solution.py:27
  425.0 47.8 %copy-start.21 = (f32[1920,512]{0,1:T(8,128)}, f32[1920,512]{0,1:T(8,128)S(1)}, u32[]{:S(2)}) copy-start(f32[1920,512]{0,1:T(8,128)S(1)} %get-tuple-element.177) | copy-start | bytes 11796484
  484.4 17.9 %collective-permute-start.2 = (bf16[6,7,512]{2,1,0:T(8,128)(2,1)S(1)}, bf16[6,7,512]{2,1,0:T(8,128)(2,1)S(1)}, u32[]{:S(2)}, u32[]{:S(2)}) collective-permute-start(bf16[6,7,512]{2,1,0:T(8,128)(2,1)S(1)} %get-tuple-element.135), channel_id=1, source_target_pairs={{0,8},{8,16},{16,24},{1,9},{9,17},{17,25},{2,10},{10,18},{18,26},{... | collective-permute-start | bytes 129032 | tf_op jit(solution)/shard_map/ppermute | solution.py:24
  489.0 13.4 %collective-permute-start.3 = (bf16[6,7,512]{2,1,0:T(8,128)(2,1)S(1)}, bf16[6,7,512]{2,1,0:T(8,128)(2,1)S(1)}, u32[]{:S(2)}, u32[]{:S(2)}) collective-permute-start(bf16[6,7,512]{2,1,0:T(8,128)(2,1)S(1)} %get-tuple-element.136), channel_id=1, source_target_pairs={{8,0},{16,8},{24,16},{9,1},{17,9},{25,17},{10,2},{18,10},{26,18},{... | collective-permute-start | bytes 129032 | tf_op jit(solution)/shard_map/ppermute | solution.py:27
  550.2 40.1 %all-to-all-start.2 = ((bf16[6,320,512]{1,0,2:T(8,128)(2,1)}), bf16[6,320,512]{1,0,2:T(8,128)(2,1)}, u32[]{:S(2)}, u32[]{:S(2)}) async-start(bf16[6,320,512]{1,0,2:T(8,128)(2,1)} %copy.211), calls=%async_computation.2 | async-start | bytes 6291456 | tf_op jit(solution)/shard_map/all_to_all | solution.py:293
  648.6 39.8 %all-to-all-start.3 = ((bf16[6,1280,128]{2,0,1:T(8,128)(2,1)}), bf16[6,1280,128]{2,0,1:T(8,128)(2,1)S(1)}, u32[]{:S(2)}, u32[]{:S(2)}) async-start(bf16[6,1280,128]{2,0,1:T(8,128)(2,1)} %copy.215), calls=%async_computation.3 | async-start | bytes 5242880 | tf_op jit(solution)/shard_map/all_to_all | solution.py:299
  652.4 266.6 %reduce-scatter.6.cloned.1.call-start = ((), (), s32[]{:S(2)}) async-start(), calls=%async_computation.9 | async-start | bytes 12976128 | tf_op jit(solution)/shard_map/reduce_scatter | solution.py:336
  798.0 121.1 %copy-start.29 = (bf16[1920,512]{1,0:T(8,128)(2,1)S(1)}, bf16[1920,512]{1,0:T(8,128)(2,1)}, u32[]{:S(2)}) copy-start(bf16[1920,512]{1,0:T(8,128)(2,1)} %copy-done.28) | copy-start | bytes 5898244
  798.0 152.3 %reduce-scatter.8.cloned.1.call-start = ((), (), s32[]{:S(2)}) async-start(), calls=%async_computation.10 | async-start | bytes 1802240 | tf_op jit(solution)/shard_map/reduce_scatter | solution.py:340
  919.0 78.8 %reduce-scatter.10.cloned.1.call-start = ((), (), s32[]{:S(2)}) async-start(), calls=%async_computation.12 | async-start | bytes 163840
  947.1 84.5 %all-gather.8.cloned.1.call-start = ((), (), s32[]{:S(2)}) async-start(), calls=%async_computation.11 | async-start | bytes 3244032 | tf_op jit(solution)/shard_map/all_gather | solution.py:348
  (143 other events, 1040.9 us)
Sparse Core Ops, SparseCore 0:
  10.3 38.8 all-gather.3
  51.0 112.6 all-gather.5
  798.1 120.7 reduce-scatter.5
  921.7 28.4 reduce-scatter.7
  953.1 23.8 reduce-scatter.9
  978.4 36.6 all-gather.7
where the time goes:
time: 1060 us; the launch traced here: 1050 us
  matrix products  293 us (28%)
  waiting for transfers between devices  268 us (25%)
  local copies, waits for them, and re-layouts  222 us (21%)
  other arithmetic  194 us (18%)
  blocking collectives  29.4 us (3%)
  starting transfers between devices  29.2 us (3%)
  between operations  16.4 us (2%)
    reduce_scatter x1, waiting for transfers between devices, body(): lax.psum_scatter(grad_stack.astype(jnp.bfloat16), 'rows', scatter_dimensi...  121 us
    dot_general x8, matrix products, inner_cols(): lax.dot_general(first, second, (((1,), (1,)), ((), ())), preferred_elemen...  68.7 us
    unnamed x327, local copies, waits for them, and re-layouts  55 us
    all_gather x1, waiting for transfers between devices, body(): block_stack = lax.all_gather(partial_stack, 'tm', axis=0, tiled=True)  52.3 us
    dot_general x2, matrix products, conv_local(): jnp.einsum('rck,kt->rtc', output_hat, inverse_table, precision=three_pass)  49.9 us
    dot_general x8, matrix products, inner_rows(): lax.dot_general(first, second, (((0,), (0,)), ((), ())), preferred_elemen...  46.5 us
    all_gather x1, waiting for transfers between devices, body(): partial_stack = lax.all_gather(copy_part, 'rows', axis=1, tiled=True)  39.7 us
    dot_general x8, matrix products, matmul(): return jnp.dot(first, second, preferred_element_type=jnp.float32)  38.7 us
  transfers between devices with their start and end apart: 14, of which 7 were waited for; matrix products, arithmetic and copies ran while one was open for 25% of the time, Pallas kernels for 0%

commit v1 on v0

--- a/solution.py
+++ b/solution.py
@@ -1,3 +1,4 @@
+import functools
 from functools import partial
 import math
 import jax
@@ -14,6 +15,30 @@
 three_pass = lax.Precision.HIGH
 rate_blocks = 0.1
 rate_small = 0.5
+
+
+def remake_sector_over_axis(vector, peer_axis):
+    g_now = lax.axis_size(peer_axis)
+    carry_in = lax.axis_index(peer_axis)
+    step_out, row_out, right_arr = (g_now, carry_in, vector.shape[0])
+    b_now, u_next = (vector, 1)
+    while u_next < step_out:
+        b_now = jnp.concatenate(
+            [
+                b_now,
+                lax.ppermute(
+                    b_now,
+                    peer_axis,
+                    [(hop_no, (hop_no - u_next) % step_out) for hop_no in range(step_out)],
+                ),
+            ],
+            axis=0,
+        )
+        u_next = 2 * u_next
+    return jnp.roll(b_now, shift=row_out * right_arr, axis=0)
+
+
+cells_register = functools.partial(remake_sector_over_axis, peer_axis="tm")
 
 
 def with_halo(block, sides, width):
@@ -206,7 +231,7 @@
     scaling = 1.0 / math.sqrt(token_count * lax.axis_size("tm") * lax.axis_size("rows"))
     copy_part = master.astype(jnp.bfloat16)
     partial_stack = lax.all_gather(copy_part, "rows", axis=1, tiled=True)
-    block_stack = lax.all_gather(partial_stack, "tm", axis=0, tiled=True)
+    block_stack = cells_register(partial_stack)
     ffa_in, ffa_out, ffb_in, ffb_out, mixer_in, mixer_out, conv_in, conv_out = matrices(block_stack)
     kernel_rows = small_params[5:]
     stream_zero = features.astype(jnp.float32).reshape(token_count, width)

time: 1060 us -> 1160 us (1.094)
  waiting for transfers between devices: 268 us -> 326 us
  local copies, waits for them, and re-layouts: 222 us -> 251 us
    ppermute x0 -> x2, waiting for transfers between devices: none -> 113 us  [remake_sector_over_axis(): lax.ppermute(b_now, peer_axis, [(hop_no, (hop_no - u_next) % step_out) fo...]
    all_gather x1 -> x0, waiting for transfers between devices: 52.3 us -> none  [body(): block_stack = lax.all_gather(partial_stack, 'tm', axis=0, tiled=True)]
    unnamed x327 -> x332, local copies, waits for them, and re-layouts: 55 us -> 74.3 us
  transfers between devices with their start and end apart: 14 -> 15, of which waited for: 7 -> 8; matrix products, arithmetic and copies ran while one was open for 25% -> 24% of each run, Pallas kernels for 0% -> 0%
where the time goes in v1:
time: 1160 us; the launch traced here: 1150 us
  waiting for transfers between devices  326 us (28%)
  matrix products  297 us (26%)
  local copies, waits for them, and re-layouts  251 us (22%)
  other arithmetic  200 us (17%)
  starting transfers between devices  33 us (3%)
  blocking collectives  29.3 us (3%)
  between operations  16.1 us (1%)
    reduce_scatter x1, waiting for transfers between devices, body(): lax.psum_scatter(grad_stack.astype(jnp.bfloat16), 'rows', scatter_dimensi...  119 us
    ppermute x2, waiting for transfers between devices, remake_sector_over_axis(): lax.ppermute(b_now, peer_axis, [(hop_no, (hop_no - u_next) % step_out) fo...  113 us
    unnamed x332, local copies, waits for them, and re-layouts  74.3 us
    dot_general x8, matrix products, inner_cols(): lax.dot_general(first, second, (((1,), (1,)), ((), ())), preferred_elemen...  68.9 us
    dot_general x2, matrix products, conv_local(): jnp.einsum('rck,kt->rtc', output_hat, inverse_table, precision=three_pass)  50.1 us
    dot_general x8, matrix products, inner_rows(): lax.dot_general(first, second, (((0,), (0,)), ((), ())), preferred_elemen...  46.7 us
    all_gather x1, waiting for transfers between devices, body(): partial_stack = lax.all_gather(copy_part, 'rows', axis=1, tiled=True)  39.8 us
    dot_general x8, matrix products, matmul(): return jnp.dot(first, second, preferred_element_type=jnp.float32)  38.6 us
  transfers between devices with their start and end apart: 15, of which 8 were waited for; matrix products, arithmetic and copies ran while one was open for 24% of the time, Pallas kernels for 0%

profile of v1, /device:TPU:0, one launch (start us, length us, event | category | flops | bytes accessed | tf_op | source)
XLA Modules:
  0.0 1152.0 jit_solution(14900747077311921334)
XLA Ops:
  9.2 39.8 %all-gather.3.cloned.1.call-done = bf16[22,256,256]{2,1,0:T(8,128)(2,1)} async-done(((bf16[22,32,256]{2,1,0:T(8,128)(2,1)}), bf16[22,256,256]{2,1,0:T(8,128)(2,1)}) %all-gather.3.cloned.1.call-update) | async-done | bytes 2883600 | tf_op jit(solution)/shard_map/all_gather | solution.py:233
  61.6 52.4 %collective-permute-done = bf16[22,256,256]{2,1,0:T(8,128)(2,1)} collective-permute-done((bf16[22,256,256]{2,1,0:T(8,128)(2,1)}, bf16[22,256,256]{2,1,0:T(8,128)(2,1)}, u32[]{:S(2)}, u32[]{:S(2)}) %collective-permute-start) | collective-permute-done | bytes 2883616 | tf_op jit(solution)/shard_map/ppermute | solution.py:29
  137.6 27.1 %sine_negate_fusion = (f32[1280,1280]{1,0:T(8,128)S(1)}, f32[1280,1280]{1,0:T(8,128)S(1)}) fusion(), kind=kLoop, calls=%fused_computation.60 | loop fusion | flops 16384000 | bytes 13107200 | tf_op jit(solution)/shard_map/neg | solution.py:144
  184.5 60.2 %collective-permute-done.1 = bf16[44,256,256]{2,1,0:T(8,128)(2,1)} collective-permute-done((bf16[44,256,256]{2,1,0:T(8,128)(2,1)}, bf16[44,256,256]{2,1,0:T(8,128)(2,1)}, u32[]{:S(2)}, u32[]{:S(2)}) %collective-permute-start.1) | collective-permute-done | bytes 5767200 | tf_op jit(solution)/shard_map/ppermute | solution.py:29
  280.7 9.7 multiply_convert_fusion.2
  306.4 28.6 %broadcast_multiply_fusion.1 = (f32[1280,1280]{1,0:T(8,128)}, f32[1280,1280]{1,0:T(8,128)}) fusion(f32[1280]{0:T(1024)S(1)} %select_multiply_fusion), kind=kLoop, calls=%fused_computation.185 | loop fusion | flops 19660800 | bytes 13112320 | tf_op jit(solution)/shard_map/mul | solution.py:144
  346.9 16.8 %fusion.18 = f32[6,128,5120]{2,1,0:T(8,128)} fusion(bf16[6,1280,128]{2,1,0:T(8,128)(2,1)S(1)} %bitcast.422, bf16[1280,2560]{1,0:T(8,128)(2,1)} %subtract_convert_fusion, bf16[1280,2560]{1,0:T(8,128)(2,1)} %fusion.32), kind=kOutput, calls=%fused_computation.49 | convolution fusion | flops 10092544000 | bytes 30801920 | tf_op jit(solution)/shard_map/jvp(rtc,tk->rck)/dot_general | solution.py:170
  376.6 35.8 %fusion.73 = bf16[6,1280,128]{2,1,0:T(8,128)(2,1)S(1)} fusion(f32[6,1280,128]{2,1,0:T(8,128)S(1)} %copy-done.53, f32[6,128,1280]{2,1,0:T(8,128)} %get-tuple-element.127, f32[6,128,1280]{2,1,0:T(8,128)S(1)} %get-tuple-element.126, f32[1280,1280]{1,0:T(8,128)} %get-tuple-element.169, f32[1280,1280]{1,0:T(8,128)} %get-tuple-element.168), kind=kOutput, calls=%fused_computation.137 | convolution fusion | flops 15106703360 | bytes 26869760 | tf_op jit(solution)/shard_map/jvp(rck,kt->rtc)/dot_general | solution.py:188
  430.4 23.0 %all-to-all-done.1 = bf16[6,1280,128]{2,0,1:T(8,128)(2,1)S(1)} async-done(((bf16[6,1280,128]{2,0,1:T(8,128)(2,1)}), bf16[6,1280,128]{2,0,1:T(8,128)(2,1)S(1)}, u32[]{:S(2)}, u32[]{:S(2)}) %all-to-all-start.1) | async-done | bytes 1966112 | tf_op jit(solution)/shard_map/all_to_all | solution.py:259
  508.5 8.8 multiply_convert_fusion.9
  529.3 10.1 multiply_convert_fusion.1
  550.5 14.8 %fusion.2 = bf16[1920,2048]{1,0:T(8,128)(2,1)} fusion(f32[1920,2048]{1,0:T(8,128)} %get-tuple-element.179, bf16[2048,512]{0,1:T(8,128)(2,1)S(1)} %bitcast.412, f32[1920,512]{0,1:T(8,128)S(1)} %get-tuple-element.109, f32[1920]{0:T(1024)S(1)} %negate_multiply_fusion.4), kind=kOutput, calls=%fused_computation.21 | convolution fusion | flops 4068802560 | bytes 29629952 | tf_op jit(solution)/shard_map/dot_general | solution.py:92
  661.8 9.6 fusion.120
  671.4 19.5 %all-to-all-done.2 = bf16[6,320,512]{1,0,2:T(8,128)(2,1)} async-done(((bf16[6,320,512]{1,0,2:T(8,128)(2,1)}), bf16[6,320,512]{1,0,2:T(8,128)(2,1)}, u32[]{:S(2)}, u32[]{:S(2)}) %all-to-all-start.2) | async-done | bytes 1966112 | tf_op jit(solution)/shard_map/all_to_all | solution.py:318
  700.0 14.3 %fusion.16 = f32[6,128,2560]{2,1,0:T(8,128)S(1)} fusion(f32[1280,1280]{1,0:T(8,128)} %get-tuple-element.169, f32[1280,1280]{1,0:T(8,128)} %get-tuple-element.168, bf16[6,1280,128]{1,2,0:T(8,128)(2,1)} %copy.214), kind=kOutput, calls=%fused_computation.46 | convolution fusion | flops 15102771200 | bytes 22937600 | tf_op jit(solution)/shard_map/transpose(jvp(rck,kt->rtc))/dot_general | solution.py:188
  724.5 21.4 %fusion.79 = bf16[6,1280,128]{1,2,0:T(8,128)(2,1)S(1)} fusion(bf16[1280,2560]{1,0:T(8,128)(2,1)} %subtract_convert_fusion, bf16[1280,2560]{1,0:T(8,128)(2,1)} %fusion.32, f32[6,128,2560]{2,1,0:T(8,128)} %pad_add_fusion), kind=kOutput, calls=%fused_computation.186 | convolution fusion | flops 10097459200 | bytes 22937600 | tf_op jit(solution)/shard_map/transpose(jvp(rtc,tk->rck))/dot_general | solution.py:170
  804.2 9.7 fusion.184
  824.7 17.8 %fusion.8 = (bf16[2048,1920]{0,1:T(8,128)(2,1)}, f32[1920,2048]{1,0:T(8,128)}) fusion(f32[1920,2048]{1,0:T(8,128)} %get-tuple-element.171, bf16[1920,512]{0,1:T(8,128)(2,1)S(1)} %multiply_convert_fusion.5, bf16[2048,512]{0,1:T(8,128)(2,1)S(1)} %bitcast.407), kind=kOutput, calls=%fused_computation.27 | convolution fusion | flops 4065853440 | bytes 43384832 | tf_op jit(solution)/shard_map/dot_general | solution.py:92
  842.5 10.8 copy.263
  853.3 17.3 %multiply_reduce_fusion.9 = (f32[1920]{0:T(1024)S(1)}, f32[1920,512]{0,1:T(8,128)S(1)}) fusion(f32[1920,512]{0,1:T(8,128)} %copy.178, f32[1920]{0:T(1024)S(1)} %copy-done.99, f32[512]{0:T(512)S(1)} %bitcast.439, bf16[512,2048]{1,0:T(8,128)(2,1)S(1)} %bitcast.405, f32[1920,2048]{1,0:T(8,128)} %get-tuple-element.171, f32[1920,2048]{1,0:T(8,128)} %get-tuple-element.189), kind=kOutput, calls=%fused_computation.150 | convolution fusion | flops 4069783552 | bytes 41436160 | tf_op jit(solution)/shard_map/dot_general | solution.py:92
  899.0 118.9 %reduce-scatter.6.cloned.1.call-done = bf16[88,32,256]{2,1,0:T(8,128)(2,1)} async-done(((bf16[88,256,256]{2,1,0:T(8,128)(2,1)}), bf16[88,32,256]{2,1,0:T(8,128)(2,1)}) %reduce-scatter.6.cloned.1.call-update) | async-done | bytes 1441808 | tf_op jit(solution)/shard_map/reduce_scatter | solution.py:361
  1018.1 25.6 %fusion.52 = (f32[512]{0:T(512)S(1)}, f32[512]{0:T(512)S(1)}, f32[512]{0:T(512)S(1)}, f32[512]{0:T(512)S(1)}, f32[512]{0:T(512)S(1)}, /*index=5*/f32[512]{0:T(51...) fusion(bf16[6,320,512]{2,1,0:T(8,128)(2,1)S(1)} %bitcast.352, ...), kind=kLoop, calls=%fused_computation.98 | loop fusion | flops 30466560 | bytes 60979200 | tf_op jit(solution)/shard_map/reduce_sum | solution.py:301
  1067.9 16.2 %fusion.30 = f32[128,1280]{1,0:T(8,128)S(1)} fusion(f32[1280,1280]{1,0:T(8,128)} %copy-done.2, f32[1280,1280]{1,0:T(8,128)} %copy-done.3, f32[128,1280]{1,0:T(8,128)S(1)} %add_any.121, f32[128,1280]{1,0:T(8,128)S(1)} %add_any.120), kind=kOutput, calls=%fused_computation.66 | convolution fusion | flops 5036769280 | bytes 15073280 | tf_op jit(solution)/shard_map/transpose(jvp())/dot_general | solution.py:169
  1097.9 29.3 %all-reduce.13 = (f32[20,128]{1,0:T(8,128)S(1)}, f32[2,32]{1,0:T(2,128)S(1)}, f32[2,128,32]{1,2,0:T(8,128)S(1)}) all-reduce(bf16[20,128]{1,0:T(8,128)(2,1)S(1)} %copy.265, f32[2,32]{1,0:T(2,128)S(1)} %multiply_multiply_fusion.5, f32[2,128,32]{1,2,0:T(8,128)S(1)} %add_multiply_fusion), channel_id=1, replica_groups=mesh['tm'=4,'rows'=8] {'rows'}, use_global_device_ids=true, to_apply=%region_43.44 | all-reduce | flops 10816 | bytes 81408 | tf_op jit(solution)/shard_map/psum | solution.py:370
  (525 shorter events, 498.3 us)
Async XLA Ops:
  7.2 1123.5 %copy-start = (f32[22,32,256]{2,1,0:T(8,128)S(1)}, f32[22,32,256]{2,1,0:T(8,128)}, u32[]{:S(2)}) copy-start(f32[22,32,256]{2,1,0:T(8,128)} %param.19) | copy-start | bytes 2162692
  7.2 41.9 %all-gather.3.cloned.1.call-start = ((), (), s32[]{:S(2)}) async-start(), calls=%async_computation.7 | async-start | bytes 3244032 | tf_op jit(solution)/shard_map/all_gather | solution.py:233
  49.1 64.9 %collective-permute-start = (bf16[22,256,256]{2,1,0:T(8,128)(2,1)}, bf16[22,256,256]{2,1,0:T(8,128)(2,1)}, u32[]{:S(2)}, u32[]{:S(2)}) collective-permute-start(bf16[22,256,256]{2,1,0:T(8,128)(2,1)} %all-gather.3.cloned.1.call-done), channel_id=1, source_target_pairs={{0,24},{8,0},{16,8},{24,16},{1,25},{9,1},{17,9},{25,17},{2,26},{10... | collective-permute-start | bytes 8650760 | tf_op jit(solution)/shard_map/ppermute | solution.py:29
  54.2 59.8 %copy-start.27 = (bf16[22,256,256]{2,1,0:T(8,128)(2,1)S(1)}, bf16[22,256,256]{2,1,0:T(8,128)(2,1)}, u32[]{:S(2)}) copy-start(bf16[22,256,256]{2,1,0:T(8,128)(2,1)} %all-gather.3.cloned.1.call-done) | copy-start | bytes 8650756
  56.3 78.7 %copy-start.115 = (f32[2,32]{1,0:T(2,128)}, f32[2,32]{1,0:T(2,128)S(1)}, u32[]{:S(2)}) copy-start(f32[2,32]{1,0:T(2,128)S(1)} %exponential_negate_fusion) | copy-start | bytes 772
  56.4 79.4 %copy-start.88 = (f32[6,320]{1,0:T(8,128)}, f32[6,320]{1,0:T(8,128)S(1)}, u32[]{:S(2)}) copy-start(f32[6,320]{1,0:T(8,128)S(1)} %broadcast_multiply_fusion.3) | copy-start | bytes 23044
  61.6 58.6 %copy-start.26 = (bf16[6,320,512]{2,1,0:T(8,128)(2,1)S(1)}, bf16[6,320,512]{2,1,0:T(8,128)(2,1)}, u32[]{:S(2)}) copy-start(bf16[6,320,512]{2,1,0:T(8,128)(2,1)} %param.12) | copy-start | bytes 5898244
  61.6 59.5 %copy-start.107 = (f32[20,512]{1,0:T(8,128)S(1)}, f32[20,512]{1,0:T(8,128)}, u32[]{:S(2)}) copy-start(f32[20,512]{1,0:T(8,128)} %param.21) | copy-start | bytes 122884
  118.8 125.9 %collective-permute-start.1 = (bf16[44,256,256]{2,1,0:T(8,128)(2,1)}, bf16[44,256,256]{2,1,0:T(8,128)(2,1)}, u32[]{:S(2)}, u32[]{:S(2)}) collective-permute-start(bf16[44,256,256]{2,1,0:T(8,128)(2,1)} %pad_maximum_fusion.3), channel_id=1, source_target_pairs={{0,16},{8,24},{16,0},{24,8},{1,17},{9,25},{17,1},{25,9},{2,18},{10... | collective-permute-start | bytes 17301512 | tf_op jit(solution)/shard_map/ppermute | solution.py:29
  135.0 160.4 %copy-start.117 = (f32[1,512]{1,0:T(1,128)}, f32[1,512]{1,0:T(1,128)S(1)}, u32[]{:S(2)}) copy-start(f32[1,512]{1,0:T(1,128)S(1)} %get-tuple-element.161) | copy-start | bytes 6148
  172.6 198.3 %copy-start.46 = (f32[128,1280]{1,0:T(8,128)}, f32[128,1280]{1,0:T(8,128)S(1)}, u32[]{:S(2)}) copy-start(f32[128,1280]{1,0:T(8,128)S(1)} %get-tuple-element.139) | copy-start | bytes 1966084
  301.5 40.6 %all-to-all-start = ((bf16[6,320,512]{1,0,2:T(8,128)(2,1)}), bf16[6,320,512]{1,0,2:T(8,128)(2,1)}, u32[]{:S(2)}, u32[]{:S(2)}) async-start(bf16[6,320,512]{1,0,2:T(8,128)(2,1)} %copy.180), calls=%async_computation | async-start | bytes 6291456 | tf_op jit(solution)/shard_map/all_to_all | solution.py:244
  420.9 32.6 %all-to-all-start.1 = ((bf16[6,1280,128]{2,0,1:T(8,128)(2,1)}), bf16[6,1280,128]{2,0,1:T(8,128)(2,1)S(1)}, u32[]{:S(2)}, u32[]{:S(2)}) async-start(bf16[6,1280,128]{2,0,1:T(8,128)(2,1)} %copy.192), calls=%async_computation.1 | async-start | bytes 5242880 | tf_op jit(solution)/shard_map/all_to_all | solution.py:259
  473.8 33.8 %collective-permute-start.2 = (bf16[6,7,512]{2,1,0:T(8,128)(2,1)S(1)}, bf16[6,7,512]{2,1,0:T(8,128)(2,1)S(1)}, u32[]{:S(2)}, u32[]{:S(2)}) collective-permute-start(bf16[6,7,512]{2,1,0:T(8,128)(2,1)S(1)} %get-tuple-element.137), channel_id=1, source_target_pairs={{0,8},{8,16},{16,24},{1,9},{9,17},{17,25},{2,10},{10,18},{18,26},{... | collective-permute-start | bytes 129032 | tf_op jit(solution)/shard_map/ppermute | solution.py:49
  477.3 30.3 %collective-permute-start.3 = (bf16[6,7,512]{2,1,0:T(8,128)(2,1)S(1)}, bf16[6,7,512]{2,1,0:T(8,128)(2,1)S(1)}, u32[]{:S(2)}, u32[]{:S(2)}) collective-permute-start(bf16[6,7,512]{2,1,0:T(8,128)(2,1)S(1)} %get-tuple-element.138), channel_id=1, source_target_pairs={{8,0},{16,8},{24,16},{9,1},{17,9},{25,17},{10,2},{18,10},{26,18},{... | collective-permute-start | bytes 129032 | tf_op jit(solution)/shard_map/ppermute | solution.py:52
  585.6 17.9 %collective-permute-start.4 = (bf16[6,7,512]{2,1,0:T(8,128)(2,1)S(1)}, bf16[6,7,512]{2,1,0:T(8,128)(2,1)S(1)}, u32[]{:S(2)}, u32[]{:S(2)}) collective-permute-start(bf16[6,7,512]{2,1,0:T(8,128)(2,1)S(1)} %get-tuple-element.135), channel_id=1, source_target_pairs={{0,8},{8,16},{16,24},{1,9},{9,17},{17,25},{2,10},{10,18},{18,26},{... | collective-permute-start | bytes 129032 | tf_op jit(solution)/shard_map/ppermute | solution.py:49
  590.2 13.4 %collective-permute-start.5 = (bf16[6,7,512]{2,1,0:T(8,128)(2,1)S(1)}, bf16[6,7,512]{2,1,0:T(8,128)(2,1)S(1)}, u32[]{:S(2)}, u32[]{:S(2)}) collective-permute-start(bf16[6,7,512]{2,1,0:T(8,128)(2,1)S(1)} %get-tuple-element.136), channel_id=1, source_target_pairs={{8,0},{16,8},{24,16},{9,1},{17,9},{25,17},{10,2},{18,10},{26,18},{... | collective-permute-start | bytes 129032 | tf_op jit(solution)/shard_map/ppermute | solution.py:52
  651.4 39.4 %all-to-all-start.2 = ((bf16[6,320,512]{1,0,2:T(8,128)(2,1)}), bf16[6,320,512]{1,0,2:T(8,128)(2,1)}, u32[]{:S(2)}, u32[]{:S(2)}) async-start(bf16[6,320,512]{1,0,2:T(8,128)(2,1)} %copy.211), calls=%async_computation.2 | async-start | bytes 6291456 | tf_op jit(solution)/shard_map/all_to_all | solution.py:318
  749.3 39.9 %all-to-all-start.3 = ((bf16[6,1280,128]{2,0,1:T(8,128)(2,1)}), bf16[6,1280,128]{2,0,1:T(8,128)(2,1)S(1)}, u32[]{:S(2)}, u32[]{:S(2)}) async-start(bf16[6,1280,128]{2,0,1:T(8,128)(2,1)} %copy.215), calls=%async_computation.3 | async-start | bytes 5242880 | tf_op jit(solution)/shard_map/all_to_all | solution.py:324
  753.1 264.9 %reduce-scatter.6.cloned.1.call-start = ((), (), s32[]{:S(2)}) async-start(), calls=%async_computation.8 | async-start | bytes 12976128 | tf_op jit(solution)/shard_map/reduce_scatter | solution.py:361
  899.0 119.1 %copy-start.31 = (bf16[1920,512]{1,0:T(8,128)(2,1)S(1)}, bf16[1920,512]{1,0:T(8,128)(2,1)}, u32[]{:S(2)}) copy-start(bf16[1920,512]{1,0:T(8,128)(2,1)} %copy-done.30) | copy-start | bytes 5898244
  899.0 150.4 %reduce-scatter.8.cloned.1.call-start = ((), (), s32[]{:S(2)}) async-start(), calls=%async_computation.9 | async-start | bytes 1802240 | tf_op jit(solution)/shard_map/reduce_scatter | solution.py:365
  1018.0 78.9 %reduce-scatter.10.cloned.1.call-start = ((), (), s32[]{:S(2)}) async-start(), calls=%async_computation.11 | async-start | bytes 163840
  1044.7 86.0 %all-gather.5.cloned.1.call-start = ((), (), s32[]{:S(2)}) async-start(), calls=%async_computation.10 | async-start | bytes 3244032 | tf_op jit(solution)/shard_map/all_gather | solution.py:373
  (144 other events, 1074.2 us)
Sparse Core Ops, SparseCore 0:
  10.2 38.8 all-gather.2
  899.1 118.8 reduce-scatter.5
  1020.9 28.4 reduce-scatter.7
  1052.2 23.8 reduce-scatter.9
  1077.5 36.6 all-gather.4
